TPU v7x, 32 devices: a whole 2x2x4 slice. The times are simulated.
32 devices in a mesh: row: 4 (over x, core), col: 8 (over z, y).
Axes of the slice: x: 2, y: 2, z: 4, core: 2. Of those that a mesh axis runs over, the one named last changes fastest.
Arguments:
- schur: float32 [4096, 4096], P('row', 'col'), may hold values from -6 to 6
- left_rot: float32 [8, 512, 512], P('row', 'col'), may hold values from -1 to 1, as said below
- right_rot: float32 [8, 512, 512], P('col', 'row'), may hold values from -1 to 1, as said below
- left_off: float32 [8, 512, 512], P('row', 'col'), may hold values from -1 to 1, as said below
- right_off: float32 [8, 512, 512], P('col', 'row'), may hold values from -1 to 1, as said below
Outputs:
- updated: float32 [4096, 4096], P('row', 'col')
Inputs may be any that keep to these rules, and one draw needn't show every extreme that they name: `left_rot`: each 512 x 512 block is orthogonal. `right_rot`: each 512 x 512 block is orthogonal. `left_off`: each 512 x 512 block is orthogonal. `right_off`: each 512 x 512 block is orthogonal.
All inputs are finite; a program needn't handle non-finite values.
Results may differ from a plain program's by a relative error of at most 0.00007.
Values sent between devices are 32-bit elements; how exact they have to be, the bound alone decides.
A program may use at most 64 MiB of HBM per device.

v0:
```python
import jax
import jax.numpy as jnp
from jax import lax
from jax.sharding import PartitionSpec as P


def passed_along(x, axis, by):
    size = lax.axis_size(axis)
    return lax.ppermute(x, axis, [(i, (i + by) % size) for i in range(size)])


def padded_2(cells, sides, width):
    for axis, dim in sides:
        count = lax.axis_size(axis)
        head = lax.slice_in_dim(cells, 0, width, axis=dim)
        tail = lax.slice_in_dim(cells, cells.shape[dim] - width, cells.shape[dim], axis=dim)
        cells = jnp.concatenate(
            [
                lax.ppermute(tail, axis, [(i, (i + 1) % count) for i in range(count)]),
                cells,
                lax.ppermute(head, axis, [((i + 1) % count, i) for i in range(count)]),
            ],
            axis=dim,
        )
    return cells


def apply_left(blocks, rotations):
    number = rotations.shape[0]
    window = rotations.shape[1]
    shaped = blocks.reshape(number, window, blocks.shape[1])
    result = jnp.einsum("kab,kac->kbc", rotations, shaped, precision=lax.Precision.HIGHEST)
    return result.reshape(number * window, blocks.shape[1])


def apply_right(blocks, rotations):
    number = rotations.shape[0]
    window = rotations.shape[1]
    shaped = blocks.reshape(blocks.shape[0], number, window)
    result = jnp.einsum("rka,kab->rkb", shaped, rotations, precision=lax.Precision.HIGHEST)
    return result.reshape(blocks.shape[0], number * window)


def body(schur, left_rot, right_rot, left_off, right_off):
    window = left_rot.shape[2]
    half_window = window // 2
    rows_here = schur.shape[0]
    cols_here = schur.shape[1]
    rotations = lax.all_gather(right_rot, "row", axis=1, tiled=True)
    matrix = apply_right(schur, rotations)
    rotations = lax.all_gather(left_rot, "col", axis=1, tiled=True)
    matrix = apply_left(matrix, rotations)
    rotations = lax.all_gather(right_off, "row", axis=1, tiled=True)
    following = passed_along(rotations[0][:, :half_window], "col", -1)
    padded = padded_2(matrix, (("col", 1),), half_window)
    leading = jnp.dot(
        padded[:, :window], rotations[0][:, half_window:], precision=lax.Precision.HIGHEST
    )
    middle = apply_right(padded[:, window:cols_here], rotations[1:])
    trailing = jnp.dot(
        padded[:, cols_here : cols_here + window], following, precision=lax.Precision.HIGHEST
    )
    matrix = jnp.concatenate([leading, middle, trailing], axis=1)
    rotations = lax.all_gather(left_off, "col", axis=1, tiled=True)
    following = passed_along(rotations[0][:, :half_window], "row", -1)
    padded = padded_2(matrix, (("row", 0),), half_window)
    leading = jnp.dot(
        rotations[0][:, half_window:].T, padded[:window], precision=lax.Precision.HIGHEST
    )
    middle = apply_left(padded[window:rows_here], rotations[1:])
    trailing = jnp.dot(
        following.T, padded[rows_here : rows_here + window], precision=lax.Precision.HIGHEST
    )
    return jnp.concatenate([leading, middle, trailing], axis=0)


def solution(mesh):
    return jax.shard_map(
        body,
        mesh=mesh,
        in_specs=(
            P("row", "col"),
            P("row", "col", None),
            P("col", "row", None),
            P("row", "col", None),
            P("col", "row", None),
        ),
        out_specs=P("row", "col"),
        check_vma=False,
    )
```

profile of v0, /device:TPU:1, one launch (start us, length us, event | category | flops | bytes accessed | tf_op | source)
XLA Modules:
  0.0 192.9 jit_solution(4929643086227449214)
XLA Ops:
  6.5 0.0 copy-start
  6.5 0.0 all-gather.5.cloned.1.call-start
  6.5 0.7 all-gather.5.cloned.1.call-update
  7.3 0.0 all-gather.7.cloned.1.call-start
  7.3 0.7 all-gather.7.cloned.1.call-update
  8.0 0.0 all-gather.9.cloned.1.call-start
  8.1 0.7 all-gather.9.cloned.1.call-update
  8.7 0.0 all-gather.11.cloned.1.call-start
  8.8 0.5 all-gather.11.cloned.1.call-update
  9.3 18.8 %all-gather.5.cloned.1.call-done = f32[1,512,512]{2,1,0:T(8,128)} async-done(((f32[1,128,512]{2,1,0:T(8,128)}), f32[1,512,512]{2,1,0:T(8,128)}) %all-gather.5.cloned.1.call-update) | async-done | bytes 1048592 | tf_op jit(solution)/shard_map/all_gather | solution.py:49
  28.1 0.0 copy-done
  28.1 9.3 %convolution_bitcast_fusion = f32[1024,1,512]{0,2,1:T(8,128)} fusion(f32[1024,512]{1,0:T(8,128)S(1)} %copy-done, f32[1,512,512]{2,1,0:T(8,128)} %all-gather.5.cloned.1.call-done), kind=kOutput, calls=%fused_computation.9 | convolution fusion | flops 3221225472 | bytes 5242880 | tf_op jit(solution)/shard_map/rka,kab->rkb/dot_general | solution.py:40
  37.3 3.0 %copy.7 = f32[1024,1,512]{2,0,1:T(8,128)} copy(f32[1024,1,512]{0,2,1:T(8,128)} %convolution_bitcast_fusion) | data formatting | bytes 4194304 | tf_op jit(solution)/shard_map/reshape;reshape | solution.py:31
  40.3 36.8 %all-gather.7.cloned.1.call-done = f32[2,512,512]{2,1,0:T(8,128)} async-done(((f32[2,64,512]{2,1,0:T(8,128)}), f32[2,512,512]{2,1,0:T(8,128)}) %all-gather.7.cloned.1.call-update) | async-done | bytes 2097168 | tf_op jit(solution)/shard_map/all_gather | solution.py:51
  77.1 5.8 %fusion.17 = f32[2,512,512]{1,2,0:T(8,128)S(1)} fusion(f32[2,512,512]{2,1,0:T(8,128)} %bitcast.31, f32[2,512,512]{2,1,0:T(8,128)} %all-gather.7.cloned.1.call-done), kind=kOutput, calls=%fused_computation.33 | convolution fusion | flops 3221225472 | bytes 6291456 | tf_op jit(solution)/shard_map/kab,kac->kbc/dot_general | solution.py:32
  82.8 0.0 copy-start.1
  82.8 1.4 fusion.16
  84.2 0.3 copy-done.1
  84.5 0.3 collective-permute-start
  84.8 3.9 %collective-permute-start.1 = (f32[1024,256]{1,0:T(8,128)}, f32[1024,256]{1,0:T(8,128)}, u32[]{:S(2)}, u32[]{:S(2)}) collective-permute-start(f32[1024,256]{1,0:T(8,128)} %get-tuple-element.8), channel_id=1, source_target_pairs={{1,0},{2,1},{3,2},{4,3},{5,4},{6,5},{7,6},{0,7},{9,8},{10,9},{11,1... | collective-permute-start | bytes 3145736 | tf_op jit(solution)/shard_map/ppermute | solution.py:21
  88.7 7.5 %all-gather.9.cloned.1.call-done = f32[1,512,512]{2,1,0:T(8,128)} async-done(((f32[1,128,512]{2,1,0:T(8,128)}), f32[1,512,512]{2,1,0:T(8,128)}) %all-gather.9.cloned.1.call-update) | async-done | bytes 1048592 | tf_op jit(solution)/shard_map/all_gather | solution.py:53
  96.2 1.1 slice.68
  97.3 0.0 copy-start.2
  97.3 4.2 %collective-permute-start.2 = (f32[512,256]{1,0:T(8,128)S(1)}, f32[512,256]{1,0:T(8,128)S(1)}, u32[]{:S(2)}, u32[]{:S(2)}) collective-permute-start(f32[512,256]{1,0:T(8,128)S(1)} %slice.68), channel_id=1, source_target_pairs={{0,7},{1,0},{2,1},{3,2},{4,3},{5,4},{6,5},{7,6},{8,15},{9,8},{10,9... | collective-permute-start | bytes 1572872 | tf_op jit(solution)/shard_map/ppermute | solution.py:9
  101.5 42.8 %collective-permute-done = f32[1024,256]{1,0:T(8,128)} collective-permute-done((f32[1024,256]{1,0:T(8,128)S(1)}, f32[1024,256]{1,0:T(8,128)}, u32[]{:S(2)}, u32[]{:S(2)}) %collective-permute-start) | collective-permute-done | bytes 1048608 | tf_op jit(solution)/shard_map/ppermute | solution.py:19
  144.3 3.6 %fusion.2 = f32[1024,256]{0,1:T(8,128)S(1)} fusion(f32[1024,512]{1,0:T(8,128)} %bitcast.29, f32[1024,256]{1,0:T(8,128)} %collective-permute-done, f32[512,512]{1,0:T(8,128)} %bitcast.33), kind=kOutput, calls=%fused_computation.4 | convolution fusion | flops 1611137024 | bytes 4718592 | tf_op jit(solution)/shard_map/dot_general | solution.py:56
  147.9 6.7 %collective-permute-done.2 = f32[512,256]{1,0:T(8,128)S(1)} collective-permute-done((f32[512,256]{1,0:T(8,128)S(1)}, f32[512,256]{1,0:T(8,128)S(1)}, u32[]{:S(2)}, u32[]{:S(2)}) %collective-permute-start.2) | collective-permute-done | bytes 524320 | tf_op jit(solution)/shard_map/ppermute | solution.py:9
  154.6 0.0 collective-permute-done.1
  154.6 0.0 copy-done.2
  154.6 3.3 %fusion = f32[1024,256]{0,1:T(8,128)S(1)} fusion(f32[512,256]{1,0:T(8,128)S(1)} %collective-permute-done.2, f32[1024,256]{1,0:T(8,128)} %collective-permute-done.1, f32[1024,512]{1,0:T(8,128)S(1)} %bitcast.30), kind=kOutput, calls=%fused_computation.1 | convolution fusion | flops 1611137024 | bytes 4718592 | tf_op jit(solution)/shard_map/dot_general | solution.py:60
  157.9 0.0 copy-start.3
  157.9 1.0 copy-done.3
  158.9 1.0 pad_maximum_fusion.14
  159.9 3.7 %collective-permute-start.3 = (f32[256,512]{0,1:T(8,128)}, f32[256,512]{0,1:T(8,128)}, u32[]{:S(2)}, u32[]{:S(2)}) collective-permute-start(f32[256,512]{0,1:T(8,128)} %get-tuple-element.5), channel_id=1, source_target_pairs={{0,8},{8,16},{16,24},{24,0},{1,9},{9,17},{17,25},{25,1},{2,10},{10... | collective-permute-start | bytes 1572872 | tf_op jit(solution)/shard_map/ppermute | solution.py:19
  163.6 4.1 %all-gather.11.cloned.1.call-done = f32[2,512,512]{2,1,0:T(8,128)} async-done(((f32[2,64,512]{2,1,0:T(8,128)}), f32[2,512,512]{2,1,0:T(8,128)}) %all-gather.11.cloned.1.call-update) | async-done | bytes 2097168 | tf_op jit(solution)/shard_map/all_gather | solution.py:64
  167.7 0.0 copy-start.4
  167.7 1.4 slice_bitcast_fusion.2
  169.2 1.0 collective-permute-start.5
  170.2 0.6 collective-permute-start.4
  170.8 0.0 copy-done.4
  170.8 0.0 copy-done.5
  170.9 1.9 convolution_bitcast_fusion.1
  172.7 0.0 collective-permute-done.3
  172.7 2.1 %convolution_bitcast_fusion.3 = f32[256,512]{1,0:T(8,128)S(1)} fusion(f32[256,512]{0,1:T(8,128)} %collective-permute-done.3, f32[1024,256]{0,1:T(8,128)S(1)} %copy-done.4, f32[1024,256]{0,1:T(8,128)S(1)} %fusion.2, f32[512,512]{1,0:T(8,128)S(1)} %slice_bitcast_fusion.2), kind=kOutput, calls=%fused_computation.12 | convolution fusion | flops 805830656 | bytes 3670016 | tf_op jit(solution)/shard_map/dot_general | solution.py:67
  174.9 3.3 %collective-permute-done.5 = f32[512,256]{1,0:T(8,128)S(1)} collective-permute-done((f32[512,256]{1,0:T(8,128)S(1)}, f32[512,256]{1,0:T(8,128)S(1)}, u32[]{:S(2)}, u32[]{:S(2)}) %collective-permute-start.5) | collective-permute-done | bytes 524320 | tf_op jit(solution)/shard_map/ppermute | solution.py:9
  178.2 5.6 %collective-permute-done.4 = f32[256,512]{0,1:T(8,128)S(1)} collective-permute-done((f32[256,512]{0,1:T(8,128)}, f32[256,512]{0,1:T(8,128)S(1)}, u32[]{:S(2)}, u32[]{:S(2)}) %collective-permute-start.4) | collective-permute-done | bytes 524320 | tf_op jit(solution)/shard_map/ppermute | solution.py:21
  183.8 1.1 convolution_bitcast_fusion.2
  184.9 1.5 pad_maximum_fusion.4
  (2 shorter events, 0.0 us)
Async XLA Ops:
  6.5 21.5 %copy-start = (f32[1024,512]{1,0:T(8,128)S(1)}, f32[1024,512]{1,0:T(8,128)}, u32[]{:S(2)}) copy-start(f32[1024,512]{1,0:T(8,128)} %param.5) | copy-start | bytes 6291460
  6.5 21.5 %all-gather.5.cloned.1.call-start = ((), (), s32[]{:S(2)}) async-start(), calls=%async_computation | async-start | bytes 1310720 | tf_op jit(solution)/shard_map/all_gather | solution.py:49
  7.3 69.8 %all-gather.7.cloned.1.call-start = ((), (), s32[]{:S(2)}) async-start(), calls=%async_computation.1 | async-start | bytes 2359296 | tf_op jit(solution)/shard_map/all_gather | solution.py:51
  8.0 88.2 %all-gather.9.cloned.1.call-start = ((), (), s32[]{:S(2)}) async-start(), calls=%async_computation.2 | async-start | bytes 1310720 | tf_op jit(solution)/shard_map/all_gather | solution.py:53
  8.7 159.0 %all-gather.11.cloned.1.call-start = ((), (), s32[]{:S(2)}) async-start(), calls=%async_computation.3 | async-start | bytes 2359296 | tf_op jit(solution)/shard_map/all_gather | solution.py:64
  82.8 1.7 copy-start.1
  84.5 59.8 %collective-permute-start = (f32[1024,256]{1,0:T(8,128)S(1)}, f32[1024,256]{1,0:T(8,128)}, u32[]{:S(2)}, u32[]{:S(2)}) collective-permute-start(f32[1024,256]{1,0:T(8,128)S(1)} %get-tuple-element.7), channel_id=1, source_target_pairs={{0,1},{1,2},{2,3},{3,4},{4,5},{5,6},{6,7},{7,0},{8,9},{9,10},{10,1... | collective-permute-start | bytes 3145736 | tf_op jit(solution)/shard_map/ppermute | solution.py:19
  84.8 69.9 %collective-permute-start.1 = (f32[1024,256]{1,0:T(8,128)}, f32[1024,256]{1,0:T(8,128)}, u32[]{:S(2)}, u32[]{:S(2)}) collective-permute-start(f32[1024,256]{1,0:T(8,128)} %get-tuple-element.8), channel_id=1, source_target_pairs={{1,0},{2,1},{3,2},{4,3},{5,4},{6,5},{7,6},{0,7},{9,8},{10,9},{11,1... | collective-permute-start | bytes 3145736 | tf_op jit(solution)/shard_map/ppermute | solution.py:21
  97.3 57.4 %copy-start.2 = (f32[2,512,512]{1,2,0:T(8,128)S(1)}, f32[2,512,512]{1,2,0:T(8,128)}, u32[]{:S(2)}) copy-start(f32[2,512,512]{1,2,0:T(8,128)} %copy-done.1) | copy-start | bytes 6291460
  97.3 57.3 %collective-permute-start.2 = (f32[512,256]{1,0:T(8,128)S(1)}, f32[512,256]{1,0:T(8,128)S(1)}, u32[]{:S(2)}, u32[]{:S(2)}) collective-permute-start(f32[512,256]{1,0:T(8,128)S(1)} %slice.68), channel_id=1, source_target_pairs={{0,7},{1,0},{2,1},{3,2},{4,3},{5,4},{6,5},{7,6},{8,15},{9,8},{10,9... | collective-permute-start | bytes 1572872 | tf_op jit(solution)/shard_map/ppermute | solution.py:9
  157.9 1.0 copy-start.3
  159.9 12.8 %collective-permute-start.3 = (f32[256,512]{0,1:T(8,128)}, f32[256,512]{0,1:T(8,128)}, u32[]{:S(2)}, u32[]{:S(2)}) collective-permute-start(f32[256,512]{0,1:T(8,128)} %get-tuple-element.5), channel_id=1, source_target_pairs={{0,8},{8,16},{16,24},{24,0},{1,9},{9,17},{17,25},{25,1},{2,10},{10... | collective-permute-start | bytes 1572872 | tf_op jit(solution)/shard_map/ppermute | solution.py:19
  167.7 3.1 %copy-start.4 = (f32[1024,256]{0,1:T(8,128)S(1)}, f32[1024,256]{0,1:T(8,128)}, u32[]{:S(2)}) copy-start(f32[1024,256]{0,1:T(8,128)} %copy-done.3) | copy-start | bytes 3145732
  167.7 3.1 %copy-start.5 = (f32[2,512,512]{2,1,0:T(8,128)S(1)}, f32[2,512,512]{2,1,0:T(8,128)}, u32[]{:S(2)}) copy-start(f32[2,512,512]{2,1,0:T(8,128)} %all-gather.11.cloned.1.call-done) | copy-start | bytes 6291460
  169.2 9.0 %collective-permute-start.5 = (f32[512,256]{1,0:T(8,128)S(1)}, f32[512,256]{1,0:T(8,128)S(1)}, u32[]{:S(2)}, u32[]{:S(2)}) collective-permute-start(f32[512,256]{1,0:T(8,128)S(1)} %slice.74), channel_id=1, source_target_pairs={{0,24},{8,0},{16,8},{24,16},{1,25},{9,1},{17,9},{25,17},{2,26},{10... | collective-permute-start | bytes 1572872 | tf_op jit(solution)/shard_map/ppermute | solution.py:9
  170.2 13.6 %collective-permute-start.4 = (f32[256,512]{0,1:T(8,128)}, f32[256,512]{0,1:T(8,128)S(1)}, u32[]{:S(2)}, u32[]{:S(2)}) collective-permute-start(f32[256,512]{0,1:T(8,128)} %get-tuple-element.6), channel_id=1, source_target_pairs={{8,0},{16,8},{24,16},{0,24},{9,1},{17,9},{25,17},{1,25},{10,2},{18... | collective-permute-start | bytes 1572872 | tf_op jit(solution)/shard_map/ppermute | solution.py:21
Sparse Core Ops, SparseCore 0:
  8.9 19.1 all-gather.4
  30.3 46.7 all-gather.6
  78.6 17.5 all-gather.8
  98.2 69.4 all-gather.10
where the time goes:
time: 193 us
  waiting for transfers between devices  128 us (66%)
  matrix products  27.1 us (14%)
  starting transfers between devices  13.8 us (7%)
  between operations  13.2 us (7%)
  local copies, waits for them, and re-layouts  8.15 us (4%)
  other arithmetic  2.53 us (1%)
    ppermute x2, waiting for transfers between devices, padded_2(): lax.ppermute(tail, axis, [(i, (i + 1) % count) for i in range(count)])  42.8 us
    all_gather x1, waiting for transfers between devices, body(): rotations = lax.all_gather(left_rot, 'col', axis=1, tiled=True)  36.8 us
    all_gather x1, waiting for transfers between devices, body(): rotations = lax.all_gather(right_rot, 'row', axis=1, tiled=True)  18.8 us
    ppermute x2, waiting for transfers between devices, passed_along(): return lax.ppermute(x, axis, [(i, (i + by) % size) for i in range(size)])  9.97 us
    dot_general x1, matrix products, apply_right(): jnp.einsum('rka,kab->rkb', shaped, rotations, precision=lax.Precision.HIG...  9.25 us
    dot_general x2, matrix products, apply_left(): jnp.einsum('kab,kac->kbc', rotations, shaped, precision=lax.Precision.HIG...  7.62 us
    all_gather x1, waiting for transfers between devices, body(): rotations = lax.all_gather(right_off, 'row', axis=1, tiled=True)  7.54 us
    ppermute x2, waiting for transfers between devices, padded_2(): lax.ppermute(head, axis, [((i + 1) % count, i) for i in range(count)])  5.62 us
  transfers between devices with their start and end apart: 10, of which 8 were waited for; matrix products, arithmetic and copies ran while one was open for 18% of the time, Pallas kernels for 0%

commit v1 on v0

--- a/solution.py
+++ b/solution.py
@@ -2,6 +2,13 @@
 import jax.numpy as jnp
 from jax import lax
 from jax.sharding import PartitionSpec as P
+from jax.lax import axis_index, axis_size, ppermute
+
+
+def _part_leaves(obj, axis_k):
+    before = list(obj.shape[1:])
+    before[axis_k] *= obj.shape[0]
+    return jnp.moveaxis(obj, 0, axis_k).reshape(before)
 
 
 def passed_along(x, axis, by):
@@ -46,7 +53,19 @@
     half_window = window // 2
     rows_here = schur.shape[0]
     cols_here = schur.shape[1]
-    rotations = lax.all_gather(right_rot, "row", axis=1, tiled=True)
+    parts_n = axis_size("row")
+    inbox = [(j, (j + 1) % parts_n) for j in range(parts_n)]
+    buffer = [(u, tick) for tick, u in inbox]
+    n_now, inter = ([], [])
+    for dev_j in range(parts_n - 1):
+        if dev_j % 2 == 0:
+            n_now.append(ppermute(n_now[-1] if n_now else right_rot, "row", inbox))
+        else:
+            inter.append(ppermute(inter[-1] if inter else right_rot, "row", buffer))
+    arr_next = jnp.stack([*n_now[::-1], right_rot, *inter], axis=0)
+    earlier = axis_index("row") - len(n_now)
+    arr_next = arr_next[(jnp.arange(parts_n) - earlier) % parts_n]
+    rotations = _part_leaves(arr_next, 1)
     matrix = apply_right(schur, rotations)
     rotations = lax.all_gather(left_rot, "col", axis=1, tiled=True)
     matrix = apply_left(matrix, rotations)

time: 193 us -> 175 us (0.907)
  waiting for transfers between devices: 128 us -> 102 us
  starting transfers between devices: 13.8 us -> 18.8 us
  other arithmetic: 2.53 us -> 4.57 us
    all_gather x1 -> x0, waiting for transfers between devices: 18.8 us -> none  [body(): rotations = lax.all_gather(right_rot, 'row', axis=1, tiled=True)]
    all_gather x1, waiting for transfers between devices: 36.8 us -> 20.5 us  [body(): rotations = lax.all_gather(left_rot, 'col', axis=1, tiled=True)]
    ppermute x0 -> x3, waiting for transfers between devices: none -> 9.64 us  [the longest x2 9.64 us: body(): n_now.append(ppermute(n_now[-1] if n_now else right_rot, 'row', inbox))]
    ppermute x0 -> x3, starting transfers between devices: none -> 5.02 us  [the longest x2 5.02 us: body(): n_now.append(ppermute(n_now[-1] if n_now else right_rot, 'row', inbox))]
    another operation x0 -> x1, other arithmetic: none -> 2.02 us  [body(): arr_next = jnp.stack([*n_now[::-1], right_rot, *inter], axis=0)]
  transfers between devices with their start and end apart: 10 -> 12, of which waited for: 8 -> 9; matrix products, arithmetic and copies ran while one was open for 18% -> 21% of each run, Pallas kernels for 0% -> 0%
where the time goes in v1:
time: 175 us
  waiting for transfers between devices  102 us (58%)
  matrix products  25.8 us (15%)
  starting transfers between devices  18.8 us (11%)
  between operations  13.2 us (8%)
  local copies, waits for them, and re-layouts  9.95 us (6%)
  other arithmetic  4.57 us (3%)
    ppermute x2, waiting for transfers between devices, padded_2(): lax.ppermute(tail, axis, [(i, (i + 1) % count) for i in range(count)])  42.8 us
    all_gather x1, waiting for transfers between devices, body(): rotations = lax.all_gather(left_rot, 'col', axis=1, tiled=True)  20.5 us
    ppermute x2, waiting for transfers between devices, passed_along(): return lax.ppermute(x, axis, [(i, (i + by) % size) for i in range(size)])  9.99 us
    ppermute x2, waiting for transfers between devices, body(): n_now.append(ppermute(n_now[-1] if n_now else right_rot, 'row', inbox))  9.64 us
    dot_general x1, matrix products, apply_right(): jnp.einsum('rka,kab->rkb', shaped, rotations, precision=lax.Precision.HIG...  8.03 us
    dot_general x2, matrix products, apply_left(): jnp.einsum('kab,kac->kbc', rotations, shaped, precision=lax.Precision.HIG...  7.62 us
    all_gather x1, waiting for transfers between devices, body(): rotations = lax.all_gather(right_off, 'row', axis=1, tiled=True)  7.53 us
    ppermute x2, waiting for transfers between devices, padded_2(): lax.ppermute(head, axis, [((i + 1) % count, i) for i in range(count)])  5.62 us
  transfers between devices with their start and end apart: 12, of which 9 were waited for; matrix products, arithmetic and copies ran while one was open for 21% of the time, Pallas kernels for 0%

profile of v1, /device:TPU:1, one launch (start us, length us, event | category | flops | bytes accessed | tf_op | source)
XLA Modules:
  0.0 174.6 jit_solution(14104615874621838802)
XLA Ops:
  6.5 0.0 copy-start
  6.5 0.7 all-gather.4.cloned.1.call-update
  7.3 0.0 all-gather.6.cloned.1.call-start
  7.3 0.7 all-gather.6.cloned.1.call-update
  8.0 0.0 all-gather.8.cloned.1.call-start
  8.1 0.7 all-gather.8.cloned.1.call-update
  8.7 2.6 %collective-permute-start = (f32[1,128,512]{2,1,0:T(8,128)}, f32[1,128,512]{2,1,0:T(8,128)S(1)}, u32[]{:S(2)}, u32[]{:S(2)}) collective-permute-start(f32[1,128,512]{2,1,0:T(8,128)} %param.7), channel_id=1, source_target_pairs={{0,8},{8,16},{16,24},{24,0},{1,9},{9,17},{17,25},{25,1},{2,10},{10... | collective-permute-start | bytes 786440 | tf_op jit(solution)/shard_map/ppermute | solution.py:62
  11.4 0.0 collective-permute-start.2
  11.4 6.4 %collective-permute-done = f32[1,128,512]{2,1,0:T(8,128)S(1)} collective-permute-done((f32[1,128,512]{2,1,0:T(8,128)}, f32[1,128,512]{2,1,0:T(8,128)S(1)}, u32[]{:S(2)}, u32[]{:S(2)}) %collective-permute-start) | collective-permute-done | bytes 262176 | tf_op jit(solution)/shard_map/ppermute | solution.py:62
  17.7 2.4 %collective-permute-start.1 = (f32[1,128,512]{2,1,0:T(8,128)S(1)}, f32[1,128,512]{2,1,0:T(8,128)S(1)}, u32[]{:S(2)}, u32[]{:S(2)}) collective-permute-start(f32[1,128,512]{2,1,0:T(8,128)S(1)} %collective-permute-done), channel_id=1, source_target_pairs={{0,8},{8,16},{16,24},{24,0},{1,9},{9,17},{17,25},{25,1},{2,10},{10... | collective-permute-start | bytes 786440 | tf_op jit(solution)/shard_map/ppermute | solution.py:62
  20.1 0.0 collective-permute-done.2
  20.2 3.3 %collective-permute-done.1 = f32[1,128,512]{2,1,0:T(8,128)S(1)} collective-permute-done((f32[1,128,512]{2,1,0:T(8,128)S(1)}, f32[1,128,512]{2,1,0:T(8,128)S(1)}, u32[]{:S(2)}, u32[]{:S(2)}) %collective-permute-start.1) | collective-permute-done | bytes 262176 | tf_op jit(solution)/shard_map/ppermute | solution.py:62
  23.4 2.0 %maximum_bitcast_fusion = f32[4,128,512]{2,1,0:T(8,128)} fusion(f32[1,1,128,512]{3,2,1,0:T(8,128)S(1)} %bitcast.44, f32[1,1,128,512]{3,2,1,0:T(8,128)} %bitcast.42, f32[1,1,128,512]{3,2,1,0:T(8,128)S(1)} %bitcast.43, f32[1,1,128,512]{3,2,1,0:T(8,128)S(1)} %bitcast.45), kind=kLoop, calls=%fused_computation.23 | loop fusion | flops 786432 | bytes 2097152 | tf_op jit(solution)/shard_map/stack | solution.py:65
  25.5 1.8 %gather_fusion = f32[4,128,512]{2,1,0:T(8,128)S(1)} fusion(f32[4,128,512]{2,1,0:T(8,128)} %maximum_bitcast_fusion, s32[1024]{0:T(1024)S(1)} %pad_clamp_fusion), kind=kCustom, calls=%fused_computation | custom fusion | bytes 2097168 | tf_op jit(solution)/shard_map/gather | solution.py:67
  27.3 8.0 %convolution_bitcast_fusion = f32[1024,1,512]{0,2,1:T(8,128)} fusion(f32[512,512]{1,0:T(8,128)S(1)} %bitcast.39, f32[1024,512]{1,0:T(8,128)S(1)} %copy-done), kind=kOutput, calls=%fused_computation.10 | convolution fusion | flops 3221225472 | bytes 5242880 | tf_op jit(solution)/shard_map/rka,kab->rkb/dot_general | solution.py:47
  35.3 2.9 %copy.7 = f32[1024,1,512]{2,0,1:T(8,128)} copy(f32[1024,1,512]{0,2,1:T(8,128)} %convolution_bitcast_fusion) | data formatting | bytes 4194304 | tf_op jit(solution)/shard_map/reshape;reshape | solution.py:38
  38.3 20.5 %all-gather.4.cloned.1.call-done = f32[2,512,512]{2,1,0:T(8,128)} async-done(((f32[2,64,512]{2,1,0:T(8,128)}), f32[2,512,512]{2,1,0:T(8,128)}) %all-gather.4.cloned.1.call-update) | async-done | bytes 2097168 | tf_op jit(solution)/shard_map/all_gather | solution.py:70
  58.8 5.8 %fusion.18 = f32[2,512,512]{1,2,0:T(8,128)S(1)} fusion(f32[2,512,512]{2,1,0:T(8,128)} %bitcast.38, f32[2,512,512]{2,1,0:T(8,128)} %all-gather.4.cloned.1.call-done), kind=kOutput, calls=%fused_computation.41 | convolution fusion | flops 3221225472 | bytes 6291456 | tf_op jit(solution)/shard_map/kab,kac->kbc/dot_general | solution.py:39
  64.5 0.0 copy-start.1
  64.5 1.4 fusion.17
  65.9 0.3 copy-done.1
  66.2 0.3 collective-permute-start.3
  66.5 3.9 %collective-permute-start.4 = (f32[1024,256]{1,0:T(8,128)}, f32[1024,256]{1,0:T(8,128)}, u32[]{:S(2)}, u32[]{:S(2)}) collective-permute-start(f32[1024,256]{1,0:T(8,128)} %get-tuple-element.8), channel_id=1, source_target_pairs={{1,0},{2,1},{3,2},{4,3},{5,4},{6,5},{7,6},{0,7},{9,8},{10,9},{11,1... | collective-permute-start | bytes 3145736 | tf_op jit(solution)/shard_map/ppermute | solution.py:28
  70.4 7.5 %all-gather.6.cloned.1.call-done = f32[1,512,512]{2,1,0:T(8,128)} async-done(((f32[1,128,512]{2,1,0:T(8,128)}), f32[1,512,512]{2,1,0:T(8,128)}) %all-gather.6.cloned.1.call-update) | async-done | bytes 1048592 | tf_op jit(solution)/shard_map/all_gather | solution.py:72
  77.9 1.1 slice.70
  79.0 0.0 copy-start.2
  79.0 4.2 %collective-permute-start.5 = (f32[512,256]{1,0:T(8,128)S(1)}, f32[512,256]{1,0:T(8,128)S(1)}, u32[]{:S(2)}, u32[]{:S(2)}) collective-permute-start(f32[512,256]{1,0:T(8,128)S(1)} %slice.70), channel_id=1, source_target_pairs={{0,7},{1,0},{2,1},{3,2},{4,3},{5,4},{6,5},{7,6},{8,15},{9,8},{10,9... | collective-permute-start | bytes 1572872 | tf_op jit(solution)/shard_map/ppermute | solution.py:16
  83.2 42.8 %collective-permute-done.3 = f32[1024,256]{1,0:T(8,128)} collective-permute-done((f32[1024,256]{1,0:T(8,128)S(1)}, f32[1024,256]{1,0:T(8,128)}, u32[]{:S(2)}, u32[]{:S(2)}) %collective-permute-start.3) | collective-permute-done | bytes 1048608 | tf_op jit(solution)/shard_map/ppermute | solution.py:26
  126.0 3.6 %fusion.2 = f32[1024,256]{0,1:T(8,128)S(1)} fusion(f32[1024,512]{1,0:T(8,128)} %bitcast.36, f32[1024,256]{1,0:T(8,128)} %collective-permute-done.3, f32[512,512]{1,0:T(8,128)} %bitcast.41), kind=kOutput, calls=%fused_computation.5 | convolution fusion | flops 1611137024 | bytes 4718592 | tf_op jit(solution)/shard_map/dot_general | solution.py:75
  129.6 6.7 %collective-permute-done.5 = f32[512,256]{1,0:T(8,128)S(1)} collective-permute-done((f32[512,256]{1,0:T(8,128)S(1)}, f32[512,256]{1,0:T(8,128)S(1)}, u32[]{:S(2)}, u32[]{:S(2)}) %collective-permute-start.5) | collective-permute-done | bytes 524320 | tf_op jit(solution)/shard_map/ppermute | solution.py:16
  136.3 0.0 collective-permute-done.4
  136.3 3.3 %fusion = f32[1024,256]{0,1:T(8,128)S(1)} fusion(f32[512,256]{1,0:T(8,128)S(1)} %collective-permute-done.5, f32[1024,256]{1,0:T(8,128)} %collective-permute-done.4, f32[1024,512]{1,0:T(8,128)S(1)} %bitcast.37), kind=kOutput, calls=%fused_computation.2 | convolution fusion | flops 1611137024 | bytes 4718592 | tf_op jit(solution)/shard_map/dot_general | solution.py:79
  139.6 0.0 copy-start.3
  139.6 1.0 copy-done.3
  140.6 1.0 pad_maximum_fusion.14
  141.6 3.7 %collective-permute-start.6 = (f32[256,512]{0,1:T(8,128)}, f32[256,512]{0,1:T(8,128)}, u32[]{:S(2)}, u32[]{:S(2)}) collective-permute-start(f32[256,512]{0,1:T(8,128)} %get-tuple-element.5), channel_id=1, source_target_pairs={{0,8},{8,16},{16,24},{24,0},{1,9},{9,17},{17,25},{25,1},{2,10},{10... | collective-permute-start | bytes 1572872 | tf_op jit(solution)/shard_map/ppermute | solution.py:26
  145.4 4.1 %all-gather.8.cloned.1.call-done = f32[2,512,512]{2,1,0:T(8,128)} async-done(((f32[2,64,512]{2,1,0:T(8,128)}), f32[2,512,512]{2,1,0:T(8,128)}) %all-gather.8.cloned.1.call-update) | async-done | bytes 2097168 | tf_op jit(solution)/shard_map/all_gather | solution.py:83
  149.4 1.4 slice_bitcast_fusion.2
  150.9 1.0 collective-permute-start.8
  151.9 0.6 collective-permute-start.7
  152.5 0.0 copy-done.4
  152.6 1.9 %convolution_bitcast_fusion.1 = f32[512,512]{1,0:T(8,128)S(1)} fusion(f32[1024,256]{0,1:T(8,128)S(1)} %fusion.2, f32[1024,256]{0,1:T(8,128)S(1)} %copy-done.4, f32[2,512,512]{2,1,0:T(8,128)S(1)} %copy-done.5), kind=kOutput, calls=%fused_computation.11 | convolution fusion | flops 1610874880 | bytes 4194304 | tf_op jit(solution)/shard_map/kab,kac->kbc/dot_general | solution.py:39
  154.4 0.0 collective-permute-done.6
  154.4 2.1 %convolution_bitcast_fusion.3 = f32[256,512]{1,0:T(8,128)S(1)} fusion(f32[256,512]{0,1:T(8,128)} %collective-permute-done.6, f32[1024,256]{0,1:T(8,128)S(1)} %copy-done.4, f32[1024,256]{0,1:T(8,128)S(1)} %fusion.2, f32[512,512]{1,0:T(8,128)S(1)} %slice_bitcast_fusion.2), kind=kOutput, calls=%fused_computation.13 | convolution fusion | flops 805830656 | bytes 3670016 | tf_op jit(solution)/shard_map/dot_general | solution.py:86
  156.6 3.3 %collective-permute-done.8 = f32[512,256]{1,0:T(8,128)S(1)} collective-permute-done((f32[512,256]{1,0:T(8,128)S(1)}, f32[512,256]{1,0:T(8,128)S(1)}, u32[]{:S(2)}, u32[]{:S(2)}) %collective-permute-start.8) | collective-permute-done | bytes 524320 | tf_op jit(solution)/shard_map/ppermute | solution.py:16
  159.9 5.6 %collective-permute-done.7 = f32[256,512]{0,1:T(8,128)S(1)} collective-permute-done((f32[256,512]{0,1:T(8,128)}, f32[256,512]{0,1:T(8,128)S(1)}, u32[]{:S(2)}, u32[]{:S(2)}) %collective-permute-start.7) | collective-permute-done | bytes 524320 | tf_op jit(solution)/shard_map/ppermute | solution.py:28
  165.5 1.1 convolution_bitcast_fusion.2
  166.6 1.5 pad_maximum_fusion.4
  (9 shorter events, 0.1 us)
Async XLA Ops:
  6.5 20.8 %copy-start = (f32[1024,512]{1,0:T(8,128)S(1)}, f32[1024,512]{1,0:T(8,128)}, u32[]{:S(2)}) copy-start(f32[1024,512]{1,0:T(8,128)} %param.5) | copy-start | bytes 6291460
  6.5 52.2 %all-gather.4.cloned.1.call-start = ((), (), s32[]{:S(2)}) async-start(), calls=%async_computation | async-start | bytes 2359296 | tf_op jit(solution)/shard_map/all_gather | solution.py:70
  7.3 70.6 %all-gather.6.cloned.1.call-start = ((), (), s32[]{:S(2)}) async-start(), calls=%async_computation.1 | async-start | bytes 1310720 | tf_op jit(solution)/shard_map/all_gather | solution.py:72
  8.0 141.4 %all-gather.8.cloned.1.call-start = ((), (), s32[]{:S(2)}) async-start(), calls=%async_computation.2 | async-start | bytes 2359296 | tf_op jit(solution)/shard_map/all_gather | solution.py:83
  8.7 9.0 %collective-permute-start = (f32[1,128,512]{2,1,0:T(8,128)}, f32[1,128,512]{2,1,0:T(8,128)S(1)}, u32[]{:S(2)}, u32[]{:S(2)}) collective-permute-start(f32[1,128,512]{2,1,0:T(8,128)} %param.7), channel_id=1, source_target_pairs={{0,8},{8,16},{16,24},{24,0},{1,9},{9,17},{17,25},{25,1},{2,10},{10... | collective-permute-start | bytes 786440 | tf_op jit(solution)/shard_map/ppermute | solution.py:62
  11.4 8.8 %collective-permute-start.2 = (f32[1,128,512]{2,1,0:T(8,128)}, f32[1,128,512]{2,1,0:T(8,128)S(1)}, u32[]{:S(2)}, u32[]{:S(2)}) collective-permute-start(f32[1,128,512]{2,1,0:T(8,128)} %param.7), channel_id=1, source_target_pairs={{8,0},{16,8},{24,16},{0,24},{9,1},{17,9},{25,17},{1,25},{10,2},{18... | collective-permute-start | bytes 786440 | tf_op jit(solution)/shard_map/ppermute | solution.py:64
  17.7 5.7 %collective-permute-start.1 = (f32[1,128,512]{2,1,0:T(8,128)S(1)}, f32[1,128,512]{2,1,0:T(8,128)S(1)}, u32[]{:S(2)}, u32[]{:S(2)}) collective-permute-start(f32[1,128,512]{2,1,0:T(8,128)S(1)} %collective-permute-done), channel_id=1, source_target_pairs={{0,8},{8,16},{16,24},{24,0},{1,9},{9,17},{17,25},{25,1},{2,10},{10... | collective-permute-start | bytes 786440 | tf_op jit(solution)/shard_map/ppermute | solution.py:62
  64.5 1.7 copy-start.1
  66.2 59.8 %collective-permute-start.3 = (f32[1024,256]{1,0:T(8,128)S(1)}, f32[1024,256]{1,0:T(8,128)}, u32[]{:S(2)}, u32[]{:S(2)}) collective-permute-start(f32[1024,256]{1,0:T(8,128)S(1)} %get-tuple-element.7), channel_id=1, source_target_pairs={{0,1},{1,2},{2,3},{3,4},{4,5},{5,6},{6,7},{7,0},{8,9},{9,10},{10,1... | collective-permute-start | bytes 3145736 | tf_op jit(solution)/shard_map/ppermute | solution.py:26
  66.5 69.9 %collective-permute-start.4 = (f32[1024,256]{1,0:T(8,128)}, f32[1024,256]{1,0:T(8,128)}, u32[]{:S(2)}, u32[]{:S(2)}) collective-permute-start(f32[1024,256]{1,0:T(8,128)} %get-tuple-element.8), channel_id=1, source_target_pairs={{1,0},{2,1},{3,2},{4,3},{5,4},{6,5},{7,6},{0,7},{9,8},{10,9},{11,1... | collective-permute-start | bytes 3145736 | tf_op jit(solution)/shard_map/ppermute | solution.py:28
  79.0 57.4 %copy-start.2 = (f32[2,512,512]{1,2,0:T(8,128)S(1)}, f32[2,512,512]{1,2,0:T(8,128)}, u32[]{:S(2)}) copy-start(f32[2,512,512]{1,2,0:T(8,128)} %copy-done.1) | copy-start | bytes 6291460
  79.0 57.3 %collective-permute-start.5 = (f32[512,256]{1,0:T(8,128)S(1)}, f32[512,256]{1,0:T(8,128)S(1)}, u32[]{:S(2)}, u32[]{:S(2)}) collective-permute-start(f32[512,256]{1,0:T(8,128)S(1)} %slice.70), channel_id=1, source_target_pairs={{0,7},{1,0},{2,1},{3,2},{4,3},{5,4},{6,5},{7,6},{8,15},{9,8},{10,9... | collective-permute-start | bytes 1572872 | tf_op jit(solution)/shard_map/ppermute | solution.py:16
  139.6 1.0 copy-start.3
  141.6 12.8 %collective-permute-start.6 = (f32[256,512]{0,1:T(8,128)}, f32[256,512]{0,1:T(8,128)}, u32[]{:S(2)}, u32[]{:S(2)}) collective-permute-start(f32[256,512]{0,1:T(8,128)} %get-tuple-element.5), channel_id=1, source_target_pairs={{0,8},{8,16},{16,24},{24,0},{1,9},{9,17},{17,25},{25,1},{2,10},{10... | collective-permute-start | bytes 1572872 | tf_op jit(solution)/shard_map/ppermute | solution.py:26
  149.4 3.1 %copy-start.4 = (f32[1024,256]{0,1:T(8,128)S(1)}, f32[1024,256]{0,1:T(8,128)}, u32[]{:S(2)}) copy-start(f32[1024,256]{0,1:T(8,128)} %copy-done.3) | copy-start | bytes 3145732
  149.4 3.1 %copy-start.5 = (f32[2,512,512]{2,1,0:T(8,128)S(1)}, f32[2,512,512]{2,1,0:T(8,128)}, u32[]{:S(2)}) copy-start(f32[2,512,512]{2,1,0:T(8,128)} %all-gather.8.cloned.1.call-done) | copy-start | bytes 6291460
  150.9 9.0 %collective-permute-start.8 = (f32[512,256]{1,0:T(8,128)S(1)}, f32[512,256]{1,0:T(8,128)S(1)}, u32[]{:S(2)}, u32[]{:S(2)}) collective-permute-start(f32[512,256]{1,0:T(8,128)S(1)} %slice.76), channel_id=1, source_target_pairs={{0,24},{8,0},{16,8},{24,16},{1,25},{9,1},{17,9},{25,17},{2,26},{10... | collective-permute-start | bytes 1572872 | tf_op jit(solution)/shard_map/ppermute | solution.py:16
  151.9 13.6 %collective-permute-start.7 = (f32[256,512]{0,1:T(8,128)}, f32[256,512]{0,1:T(8,128)S(1)}, u32[]{:S(2)}, u32[]{:S(2)}) collective-permute-start(f32[256,512]{0,1:T(8,128)} %get-tuple-element.6), channel_id=1, source_target_pairs={{8,0},{16,8},{24,16},{0,24},{9,1},{17,9},{25,17},{1,25},{10,2},{18... | collective-permute-start | bytes 1572872 | tf_op jit(solution)/shard_map/ppermute | solution.py:28
Sparse Core Ops, SparseCore 0:
  9.5 49.2 all-gather.3
  60.3 17.5 all-gather.5
  80.1 69.2 all-gather.7
